TPU v7x, 512 devices: a whole 4x8x8 slice. The times are simulated.
512 devices in a mesh: tm: 32 (over y, z_lo, core), chan: 16 (over z_hi, x).
Axes of the slice: x: 4, y: 8, z: 8 (z_hi: 4, z_lo: 2; z = z_hi * 2 + z_lo), core: 2. Of those that a mesh axis runs over, the one named last changes fastest.
Arguments:
- record: bfloat16 [2048, 49152], P('chan', 'tm'), may hold values from -250 to 250
- offsets: int32 [4], replicated, may hold values from 0 to 37152, as said below
- dead_mask: int32 [2048], P('chan'), may hold values 0 or 1
- sources: int32 [128], replicated, may hold values from 0 to 2047
Outputs:
- cross_spectra: float32 [640, 2, 128, 2048], P('tm', None, None, 'chan')
Inputs may be any that keep to these rules, and one draw needn't show every extreme that they name: offsets[w] lies between w * 12000 and w * 12000 + 49152 - 4 * 12000; offsets[0] is 0 and the last window ends at the record's last sample.
All inputs are finite; a program needn't handle non-finite values. No bound on the sum of `dead_mask` on one device may be relied on, other than what follows from the above.
Results may differ from a plain program's by a relative error of at most 0.002.
The roundings to bfloat16 on the way count: a program that leaves them out, or rounds other values in their place, can miss the bound.
Values may be sent and summed in bfloat16 or wider, within the bound.
A program may use at most 128 MiB of HBM per device.

v0:
```python
import math
import jax
import jax.numpy as jnp
from jax import lax
from jax.sharding import PartitionSpec as P

W = 12000
F = 640
FLO = 6
NWIN = 4


def band_basis(first_bin, width, times):
    bins = first_bin + jnp.arange(width, dtype=jnp.int32)
    phase = times[:, None] * bins[None, :] % W
    angle = phase.astype(jnp.float32) * (2.0 * math.pi / W)
    return jnp.stack([jnp.cos(angle), -jnp.sin(angle)], axis=-1)


def amplitude(fourier_coefficients):
    return jnp.sqrt(fourier_coefficients[:, :, 0] ** 2 + fourier_coefficients[:, :, 1] ** 2)


def whiten(fourier_coefficients, magnitude, level):
    denominator = magnitude + 0.1 * level[None] + 1e-06
    return (fourier_coefficients / denominator[:, :, None, :]).astype(jnp.bfloat16)


def shards(record, offsets, dead_mask, sources):
    tm_count = lax.axis_size("tm")
    bins_dev = F // tm_count
    channels = record.shape[0]
    group_first = lax.axis_index("tm") * record.shape[1]
    local_times = group_first + jnp.arange(record.shape[1], dtype=jnp.int32)
    start = jnp.int32(0)
    blocks = []
    for first in range(0, lax.axis_size("tm") * bins_dev, 64):
        width = min(64, lax.axis_size("tm") * bins_dev - first)
        per_window = []
        for window in range(NWIN):
            shifted = local_times - offsets[window]
            inside = (shifted >= 0) & (shifted < W)
            basis = band_basis(FLO + start + first, width, jnp.where(inside, shifted, 0))
            basis = (basis * inside[:, None, None].astype(jnp.float32)).astype(jnp.bfloat16)
            per_window.append(
                jnp.einsum("ct,tfp->fpc", record, basis, preferred_element_type=jnp.float32)
            )
        blocks.append(jnp.stack(per_window, axis=1))
    fourier_coefficients = lax.psum_scatter(
        jnp.concatenate(blocks, axis=0), "tm", scatter_dimension=0, tiled=True
    )
    magnitude = amplitude(fourier_coefficients)
    level = lax.psum(jnp.sum(magnitude, axis=0), "tm") / F
    white = whiten(fourier_coefficients, magnitude, level)
    white = white * dead_mask.astype(jnp.bfloat16)[None, None, None, :]
    local_index = sources - lax.axis_index("chan") * channels
    onehot = (jnp.arange(channels, dtype=jnp.int32)[:, None] == local_index[None, :]).astype(
        jnp.bfloat16
    )
    selected_bins = jnp.einsum("fwpc,cs->fwps", white, onehot, preferred_element_type=jnp.float32)
    source_spec = lax.psum(selected_bins.astype(jnp.bfloat16), "chan")
    left_channel = source_spec.reshape(bins_dev, NWIN * 2, source_spec.shape[3])
    right_channel_real = white.reshape(bins_dev, NWIN * 2, channels)
    right_channel_imaginary = jnp.concatenate(
        [white[:, :, 1:2], -white[:, :, 0:1]], axis=2
    ).reshape(bins_dev, NWIN * 2, channels)
    real_component = jnp.einsum(
        "qia,qie->qae", left_channel, right_channel_real, preferred_element_type=jnp.float32
    )
    imaginary_component = jnp.einsum(
        "qia,qie->qae", left_channel, right_channel_imaginary, preferred_element_type=jnp.float32
    )
    return jnp.stack([real_component, imaginary_component], axis=1) / NWIN


def solution(mesh):
    return jax.shard_map(
        shards,
        mesh=mesh,
        in_specs=(P("chan", "tm"), P(), P("chan"), P()),
        out_specs=P("tm", None, None, "chan"),
        check_vma=False,
    )
```

profile of v0, /device:TPU:32, one launch (start us, length us, event | category | flops | bytes accessed | tf_op | source)
XLA Modules:
  0.0 483.6 jit_solution(6104584640488371410)
XLA Ops:
  6.5 0.0 copy-start
  6.5 0.0 all-reduce.3.cloned.1.call-start
  6.6 1.5 fusion.474
  8.1 1.3 fusion.412
  9.4 1.3 fusion.428
  10.7 1.2 fusion.418
  12.0 1.2 fusion.430
  13.3 64.1 %fusion.202 = (f32[1536,64,1]{0,1,2:T(8,128)S(1)}, f32[1536,64,1]{0,1,2:T(8,128)S(1)}, f32[1536,64,1]{0,1,2:T(8,128)S(1)}, f32[1536,64,1]{0,1,2:T(8,128)S(1)}, f...) fusion(s32[64]{0:T(128)S(1)} %get-tuple-element.231, ...), kind=kLoop, calls=%fused_computation.288 | loop fusion | flops 39321600 | bytes 31484416 | tf_op jit(solution)/shard_map/cos | solution.py:17
  77.4 0.3 convolution_bitcast_fusion.5
  77.7 0.3 convolution_bitcast_fusion.9
  77.9 0.3 convolution_bitcast_fusion.4
  78.2 0.3 convolution_bitcast_fusion.8
  78.5 0.3 convolution_bitcast_fusion.3
  78.8 0.3 convolution_bitcast_fusion.7
  79.0 0.3 convolution_bitcast_fusion.2
  79.3 0.3 convolution_bitcast_fusion.6
  79.6 0.3 convolution_bitcast_fusion.13
  79.8 0.3 convolution_bitcast_fusion.12
  80.1 0.3 convolution_bitcast_fusion.11
  80.4 0.3 convolution_bitcast_fusion.10
  80.6 0.3 convolution_bitcast_fusion.17
  80.9 0.3 convolution_bitcast_fusion.16
  81.2 0.3 convolution_bitcast_fusion.15
  81.5 0.3 convolution_bitcast_fusion.14
  81.7 0.3 convolution_bitcast_fusion.21
  82.0 0.3 convolution_bitcast_fusion.20
  82.3 0.3 convolution_bitcast_fusion.19
  82.5 0.3 convolution_bitcast_fusion.18
  82.8 0.3 convolution_bitcast_fusion.25
  83.1 0.3 convolution_bitcast_fusion.24
  83.3 0.3 convolution_bitcast_fusion.23
  83.6 0.3 convolution_bitcast_fusion.22
  83.9 0.3 convolution_bitcast_fusion.29
  84.2 0.3 convolution_bitcast_fusion.28
  84.4 0.3 convolution_bitcast_fusion.27
  84.7 0.3 convolution_bitcast_fusion.26
  85.0 0.3 convolution_bitcast_fusion.33
  85.2 0.3 convolution_bitcast_fusion.32
  85.5 0.3 convolution_bitcast_fusion.31
  85.8 0.3 convolution_bitcast_fusion.30
  86.0 0.3 convolution_bitcast_fusion.37
  86.3 0.3 convolution_bitcast_fusion.36
  86.6 0.3 convolution_bitcast_fusion.35
  86.8 0.3 convolution_bitcast_fusion.34
  87.1 0.3 convolution_bitcast_fusion.41
  87.4 0.3 convolution_bitcast_fusion.40
  87.7 0.3 convolution_bitcast_fusion.39
  87.9 0.3 convolution_bitcast_fusion.38
  88.5 3.2 copy.14
  91.7 0.0 all-reduce.3.cloned.1.call-update
  91.7 0.6 copy-done.1
  92.3 1.3 dynamic-slice
  94.4 0.0 copy-done.2
  94.4 238.8 %all-reduce.3.cloned.1.call-done = f32[640,4,2,128]{3,1,2,0:T(4,128)} async-done(((f32[640,4,2,128]{3,1,2,0:T(4,128)}), f32[640,4,2,128]{3,1,2,0:T(4,128)}) %all-reduce.3.cloned.1.call-update) | async-done | bytes 2621456
  333.2 0.8 fusion.472
  334.0 55.1 %psum.14 = f32[4,128]{1,0:T(4,128)S(1)} all-reduce(f32[4,128]{1,0:T(4,128)S(1)} %fusion.472), channel_id=1, replica_groups=mesh['tm'=32,'chan'=16] {'tm'}, use_global_device_ids=true, to_apply=%region_2.3 | all-reduce | flops 512 | bytes 4096 | tf_op jit(solution)/shard_map/psum | solution.py:53
  389.2 0.8 add_bitcast_fusion
  390.0 0.9 fusion.406
  391.0 0.2 convolution_convert_fusion
  391.2 82.7 %psum.15 = bf16[20,8,128]{2,1,0:T(8,128)(2,1)S(1)} all-reduce(bf16[20,8,128]{2,1,0:T(8,128)(2,1)S(1)} %copy.16), channel_id=1, replica_groups=mesh['tm'=32,'chan'=16] {'chan'}, use_global_device_ids=true, to_apply=%region_3.4 | all-reduce | flops 20480 | bytes 81920 | tf_op jit(solution)/shard_map/psum | solution.py:61
  473.9 0.4 convolution_bitcast_fusion.1
  474.3 0.4 convolution_bitcast_fusion
  474.7 0.3 maximum_multiply_fusion
  475.0 1.7 copy.19
  (26 shorter events, 0.4 us)
Async XLA Ops:
  6.5 70.8 %copy-start = (bf16[128,1536]{1,0:T(8,128)(2,1)S(1)}, bf16[128,1536]{1,0:T(8,128)(2,1)}, u32[]{:S(2)}) copy-start(bf16[128,1536]{1,0:T(8,128)(2,1)} %param.4) | copy-start | bytes 1179652
  6.5 326.7 %all-reduce.3.cloned.1.call-start = ((), (), s32[]{:S(2)}) async-start(), calls=%async_computation | async-start | bytes 5242880
  91.7 0.7 copy-start.1
  91.7 2.7 copy-start.2
Sparse Core Ops, SparseCore 0:
  91.8 241.3 all-reduce.2
where the time goes:
time: 484 us
  waiting for transfers between devices  239 us (49%)
  blocking collectives  138 us (29%)
  other arithmetic  72.5 us (15%)
  between operations  14.6 us (3%)
  matrix products  11.5 us (2%)
  local copies, waits for them, and re-layouts  8.37 us (2%)
    unnamed x2, waiting for transfers between devices  239 us
    psum x1, blocking collectives, shards(): source_spec = lax.psum(selected_bins.astype(jnp.bfloat16), 'chan')  82.7 us
    cos x1, other arithmetic, band_basis(): return jnp.stack([jnp.cos(angle), -jnp.sin(angle)], axis=-1)  64.1 us
    psum x1, blocking collectives, shards(): level = lax.psum(jnp.sum(magnitude, axis=0), 'tm') / F  55.1 us
    dot_general x40, matrix products, shards(): jnp.einsum('ct,tfp->fpc', record, basis, preferred_element_type=jnp.float32)  10.5 us
  transfers between devices with their start and end apart: 1, of which 1 were waited for; matrix products, arithmetic and copies ran while one was open for 0% of the time, Pallas kernels for 0%

commit v1 on v0

--- a/solution.py
+++ b/solution.py
@@ -8,6 +8,11 @@
 F = 640
 FLO = 6
 NWIN = 4
+
+
+def draft_the_racks(array_in, axis_id):
+    v_next = lax.all_gather(array_in, axis_id).sum(axis=0)
+    return v_next
 
 
 def band_basis(first_bin, width, times):
@@ -50,7 +55,7 @@
         jnp.concatenate(blocks, axis=0), "tm", scatter_dimension=0, tiled=True
     )
     magnitude = amplitude(fourier_coefficients)
-    level = lax.psum(jnp.sum(magnitude, axis=0), "tm") / F
+    level = draft_the_racks(jnp.sum(magnitude, axis=0), "tm") / F
     white = whiten(fourier_coefficients, magnitude, level)
     white = white * dead_mask.astype(jnp.bfloat16)[None, None, None, :]
     local_index = sources - lax.axis_index("chan") * channels

time: 484 us -> 461 us (0.952)
  blocking collectives: 138 us -> 115 us
    psum x1 -> x0, blocking collectives: 55.1 us -> none  [shards(): level = lax.psum(jnp.sum(magnitude, axis=0), 'tm') / F]
    all_gather x0 -> x1, blocking collectives: none -> 31 us  [draft_the_racks(): v_next = lax.all_gather(array_in, axis_id).sum(axis=0)]
where the time goes in v1:
time: 461 us
  waiting for transfers between devices  239 us (52%)
  blocking collectives  115 us (25%)
  other arithmetic  72.5 us (16%)
  between operations  14.6 us (3%)
  matrix products  11.5 us (2%)
  local copies, waits for them, and re-layouts  8.37 us (2%)
    unnamed x2, waiting for transfers between devices  239 us
    psum x1, blocking collectives, shards(): source_spec = lax.psum(selected_bins.astype(jnp.bfloat16), 'chan')  84 us
    cos x1, other arithmetic, band_basis(): return jnp.stack([jnp.cos(angle), -jnp.sin(angle)], axis=-1)  64.1 us
    all_gather x1, blocking collectives, draft_the_racks(): v_next = lax.all_gather(array_in, axis_id).sum(axis=0)  31 us
    dot_general x40, matrix products, shards(): jnp.einsum('ct,tfp->fpc', record, basis, preferred_element_type=jnp.float32)  10.5 us
  transfers between devices with their start and end apart: 1, of which 1 were waited for; matrix products, arithmetic and copies ran while one was open for 0% of the time, Pallas kernels for 0%

profile of v1, /device:TPU:32, one launch (start us, length us, event | category | flops | bytes accessed | tf_op | source)
XLA Modules:
  0.0 460.8 jit_solution(4089145924357329478)
XLA Ops:
  6.5 0.0 copy-start
  6.5 0.0 all-reduce.3.cloned.1.call-start
  6.6 1.5 fusion.474
  8.1 1.3 fusion.412
  9.4 1.3 fusion.428
  10.7 1.2 fusion.418
  12.0 1.2 fusion.430
  13.3 64.1 %fusion.202 = (f32[1536,64,1]{0,1,2:T(8,128)S(1)}, f32[1536,64,1]{0,1,2:T(8,128)S(1)}, f32[1536,64,1]{0,1,2:T(8,128)S(1)}, f32[1536,64,1]{0,1,2:T(8,128)S(1)}, f...) fusion(s32[64]{0:T(128)S(1)} %get-tuple-element.231, ...), kind=kLoop, calls=%fused_computation.288 | loop fusion | flops 39321600 | bytes 31484416 | tf_op jit(solution)/shard_map/cos | solution.py:22
  77.4 0.3 convolution_bitcast_fusion.5
  77.7 0.3 convolution_bitcast_fusion.9
  77.9 0.3 convolution_bitcast_fusion.4
  78.2 0.3 convolution_bitcast_fusion.8
  78.5 0.3 convolution_bitcast_fusion.3
  78.8 0.3 convolution_bitcast_fusion.7
  79.0 0.3 convolution_bitcast_fusion.2
  79.3 0.3 convolution_bitcast_fusion.6
  79.6 0.3 convolution_bitcast_fusion.13
  79.8 0.3 convolution_bitcast_fusion.12
  80.1 0.3 convolution_bitcast_fusion.11
  80.4 0.3 convolution_bitcast_fusion.10
  80.6 0.3 convolution_bitcast_fusion.17
  80.9 0.3 convolution_bitcast_fusion.16
  81.2 0.3 convolution_bitcast_fusion.15
  81.5 0.3 convolution_bitcast_fusion.14
  81.7 0.3 convolution_bitcast_fusion.21
  82.0 0.3 convolution_bitcast_fusion.20
  82.3 0.3 convolution_bitcast_fusion.19
  82.5 0.3 convolution_bitcast_fusion.18
  82.8 0.3 convolution_bitcast_fusion.25
  83.1 0.3 convolution_bitcast_fusion.24
  83.3 0.3 convolution_bitcast_fusion.23
  83.6 0.3 convolution_bitcast_fusion.22
  83.9 0.3 convolution_bitcast_fusion.29
  84.2 0.3 convolution_bitcast_fusion.28
  84.4 0.3 convolution_bitcast_fusion.27
  84.7 0.3 convolution_bitcast_fusion.26
  85.0 0.3 convolution_bitcast_fusion.33
  85.2 0.3 convolution_bitcast_fusion.32
  85.5 0.3 convolution_bitcast_fusion.31
  85.8 0.3 convolution_bitcast_fusion.30
  86.0 0.3 convolution_bitcast_fusion.37
  86.3 0.3 convolution_bitcast_fusion.36
  86.6 0.3 convolution_bitcast_fusion.35
  86.8 0.3 convolution_bitcast_fusion.34
  87.1 0.3 convolution_bitcast_fusion.41
  87.4 0.3 convolution_bitcast_fusion.40
  87.7 0.3 convolution_bitcast_fusion.39
  87.9 0.3 convolution_bitcast_fusion.38
  88.5 3.2 copy.14
  91.7 0.0 all-reduce.3.cloned.1.call-update
  91.7 0.6 copy-done.1
  92.3 1.3 dynamic-slice
  94.4 0.0 copy-done.2
  94.4 238.8 %all-reduce.3.cloned.1.call-done = f32[640,4,2,128]{3,1,2,0:T(4,128)} async-done(((f32[640,4,2,128]{3,1,2,0:T(4,128)}), f32[640,4,2,128]{3,1,2,0:T(4,128)}) %all-reduce.3.cloned.1.call-update) | async-done | bytes 2621456
  333.2 0.8 fusion.472
  334.0 31.0 %all-gather.1 = f32[32,4,128]{2,1,0:T(4,128)S(1)} all-gather(f32[1,4,128]{2,1,0:T(4,128)S(1)} %bitcast.188), channel_id=2, replica_groups=mesh['tm'=32,'chan'=16] {'tm'}, dimensions={0}, use_global_device_ids=true | all-gather | bytes 67584 | tf_op jit(solution)/shard_map/all_gather | solution.py:14
  365.1 0.8 add_bitcast_fusion
  365.9 0.9 fusion.406
  366.9 0.2 convolution_convert_fusion
  367.1 84.0 %psum.7 = bf16[20,8,128]{2,1,0:T(8,128)(2,1)S(1)} all-reduce(bf16[20,8,128]{2,1,0:T(8,128)(2,1)S(1)} %copy.16), channel_id=1, replica_groups=mesh['tm'=32,'chan'=16] {'chan'}, use_global_device_ids=true, to_apply=%region_3.4 | all-reduce | flops 20480 | bytes 81920 | tf_op jit(solution)/shard_map/psum | solution.py:66
  451.1 0.4 convolution_bitcast_fusion.1
  451.5 0.4 convolution_bitcast_fusion
  451.9 0.3 maximum_multiply_fusion
  452.2 1.7 copy.19
  (27 shorter events, 0.4 us)
Async XLA Ops:
  6.5 70.8 %copy-start = (bf16[128,1536]{1,0:T(8,128)(2,1)S(1)}, bf16[128,1536]{1,0:T(8,128)(2,1)}, u32[]{:S(2)}) copy-start(bf16[128,1536]{1,0:T(8,128)(2,1)} %param.4) | copy-start | bytes 1179652
  6.5 326.7 %all-reduce.3.cloned.1.call-start = ((), (), s32[]{:S(2)}) async-start(), calls=%async_computation | async-start | bytes 5242880
  91.7 0.7 copy-start.1
  91.7 2.7 copy-start.2
Sparse Core Ops, SparseCore 0:
  91.8 241.3 all-reduce.2
